TPU v7x, 32 devices: a whole 2x2x4 slice. The times are simulated.
32 devices in a mesh: wave: 8 (over z, core), lev: 4 (over y, x).
Axes of the slice: x: 2, y: 2, z: 4, core: 2. Of those that a mesh axis runs over, the one named last changes fastest.
Arguments:
- spectrum: bfloat16 [4, 4, 2, 1280, 1280], P(None, 'lev', None, 'wave'), may hold values from -6 to 6
- legendre: bfloat16 [1280, 8, 1280], P('wave'), may hold values from -0.15625 to 0.15625
- order_of_slot: int32 [1280], replicated, may hold values from 0 to 1279, each once
- reduced_length: int32 [8], replicated, may hold values from 20 to 5136, as said below
- gauss_weight: float32 [8], P('wave'), may hold values from 2 to 6
- depart_row: int32 [2, 4, 4, 8, 5632], P(None, 'lev', None, 'wave'), may hold values from -1 to 1, as said below
- depart_col: int32 [2, 4, 4, 8, 5632], P(None, 'lev', None, 'wave'), may hold values from 0 to 5135, as said below
- depart_weight: float32 [2, 4, 4, 8, 5632], P(None, 'lev', None, 'wave'), may hold values from 0.05 to 0.5
Outputs:
- spectrum_out: bfloat16 [4, 4, 2, 1280, 1280], P(None, 'lev', None, 'wave')
Inputs may be any that keep to these rules, and one draw needn't show every extreme that they name: `reduced_length`: each latitude j has 20 + 4 i points for a cycle i with j * 160 <= i < (j + 1) * 160; the last latitude has 5136. `depart_row`: offset of the departure latitude from the arrival latitude; a departure latitude outside the window reads zeros. `depart_col`: below the reduced length of the departure latitude (of the nearest window latitude where it lies outside the window). `order_of_slot`: A permutation of the zonal orders.
All inputs are finite; a program needn't handle non-finite values.
Results may differ from a plain program's by a relative error of at most 0.02.
Values may be sent and summed in bfloat16 or wider, within the bound.
A program may use at most 128 MiB of HBM per device.

v0:
```python
import math
import jax
import jax.numpy as jnp
from jax import lax
from jax.sharding import PartitionSpec as P

BLOCK = 512
full_turn = 2.0 * math.pi


def extended_2(block, sides, width):
    for axis, dim in sides:
        count = lax.axis_size(axis)
        forward = [(i, i + 1) for i in range(count - 1)]
        backward = [(target, source) for source, target in forward]
        low = lax.ppermute(
            lax.slice_in_dim(block, block.shape[dim] - width, None, axis=dim), axis, forward
        )
        high = lax.ppermute(lax.slice_in_dim(block, 0, width, axis=dim), axis, backward)
        block = jnp.concatenate([low, block, high], axis=dim)
    return block


def base_table(length, orders, order_limit, block_width):
    offsets = jnp.arange(block_width, dtype=jnp.int32)
    phases = orders[:, None] * offsets[None, :] % length
    angles = phases.astype(jnp.float32) * (jnp.float32(full_turn) / length.astype(jnp.float32))
    active = (orders < order_limit)[:, None]
    cosine = jnp.where(active, jnp.cos(angles), 0.0)
    sine_part = jnp.where(active, -jnp.sin(angles), 0.0)
    return jnp.concatenate([cosine, sine_part], axis=0).astype(jnp.bfloat16)


def block_phases(length, orders, grid_width, block_width):
    starts = jnp.arange(grid_width // block_width, dtype=jnp.int32) * block_width
    phases = starts[:, None] * orders[None, :] % length
    angles = phases.astype(jnp.float32) * (jnp.float32(full_turn) / length.astype(jnp.float32))
    return (jnp.cos(angles), jnp.sin(angles))


def synthesize(coeffs, length, order_limit, fourier_table, cos_phase, sin_phase):
    field_count = coeffs.shape[0]
    blocks = cos_phase.shape[0]
    block_width = fourier_table.shape[1]
    real_part = coeffs[:, 0, :].astype(jnp.float32)[:, None, :]
    imag_part = coeffs[:, 1, :].astype(jnp.float32)[:, None, :]
    rot_real = real_part * cos_phase[None] - imag_part * sin_phase[None]
    rot_imag = real_part * sin_phase[None] + imag_part * cos_phase[None]
    rotated = jnp.stack([rot_real, rot_imag], axis=2).astype(jnp.bfloat16)
    rotated = rotated.reshape(field_count * blocks, -1)
    result = jnp.dot(rotated, fourier_table, preferred_element_type=jnp.float32)
    result = result.reshape(field_count, blocks * block_width)
    points = jnp.arange(blocks * block_width, dtype=jnp.int32)
    factor = 1.0 / jnp.sqrt(order_limit.astype(jnp.float32))
    return jnp.where(points[None, :] < length, result * factor, 0.0)


def analyse(newgrid, fourier_table, cos_phase, sin_phase):
    field_count = newgrid.shape[0]
    blocks = cos_phase.shape[0]
    block_width = fourier_table.shape[1]
    partial_value = lax.dot_general(
        newgrid.reshape(field_count * blocks, block_width),
        fourier_table,
        (((1,), (1,)), ((), ())),
        preferred_element_type=jnp.float32,
    )
    partial_value = partial_value.reshape(field_count, blocks, 2, -1)
    part_real = partial_value[:, :, 0, :]
    part_imag = partial_value[:, :, 1, :]
    real_sum = jnp.sum(part_real * cos_phase[None] + part_imag * sin_phase[None], axis=1)
    imag_sum = jnp.sum(part_imag * cos_phase[None] - part_real * sin_phase[None], axis=1)
    return jnp.stack([real_sum, imag_sum], axis=1)


def per_device(
    spectrum,
    legendre,
    order_of_slot,
    reduced_length,
    gauss_weight,
    depart_row,
    depart_col,
    depart_weight,
):
    own_index = lax.axis_index("wave")
    slot_count = legendre.shape[0]
    orders_total = order_of_slot.shape[0]
    variables = spectrum.shape[0]
    level_count = spectrum.shape[1]
    field_count = variables * level_count
    grid_width = depart_row.shape[-1]
    stencil = depart_row.shape[2]
    own_orders = lax.dynamic_slice_in_dim(order_of_slot, own_index * slot_count, slot_count)
    degrees = jnp.arange(legendre.shape[2], dtype=jnp.int32)
    masked = jnp.where(
        degrees[None, None, :] >= own_orders[:, None, None], legendre, jnp.zeros((), jnp.bfloat16)
    )
    length = lax.dynamic_index_in_dim(reduced_length, own_index, keepdims=False)
    order_limit = jnp.minimum(orders_total, (length - 1) // 2)
    fourier_table = base_table(length, order_of_slot, order_limit, BLOCK)
    cos_phase, sin_phase = block_phases(length, order_of_slot, grid_width, BLOCK)
    own_info = (length, order_limit, fourier_table, cos_phase, sin_phase)
    weight = gauss_weight[0]
    points = jnp.arange(grid_width, dtype=jnp.int32)
    level_base = (jnp.arange(level_count, dtype=jnp.int32) * (3 * grid_width))[:, None, None]
    spectral_state = spectrum
    for step_index in range(depart_row.shape[0]):
        fourier = jnp.einsum(
            "vlcsn,sjn->jvlcs", spectral_state, masked, preferred_element_type=jnp.float32
        ).astype(jnp.bfloat16)
        gathered = lax.all_to_all(fourier, "wave", split_axis=0, concat_axis=4, tiled=True)
        own_grid = synthesize(
            gathered.reshape(field_count, 2, orders_total),
            own_info[0],
            own_info[1],
            own_info[2],
            own_info[3],
            own_info[4],
        )
        extended = extended_2(
            own_grid.reshape(variables, level_count, 1, grid_width).astype(jnp.bfloat16),
            (("wave", 2),),
            1,
        ).astype(jnp.float32)
        flat_rows = extended.reshape(variables, level_count * 3 * grid_width)
        row_offsets = depart_row[step_index][:, :, 0, :]
        columns = depart_col[step_index][:, :, 0, :]
        weights = depart_weight[step_index][:, :, 0, :]
        flat_index = (level_base + (row_offsets + 1) * grid_width + columns).reshape(-1)
        values = jnp.take(flat_rows, flat_index, axis=1)
        values = values.reshape(variables, level_count, stencil, grid_width)
        interp = jnp.sum(values * weights[None], axis=2)
        tendency = interp + 0.5 * jnp.roll(interp, -1, axis=0) * jnp.tanh(
            jnp.roll(interp, -2, axis=0)
        )
        newgrid = jnp.where(points < own_info[0], tendency, 0.0).astype(jnp.bfloat16)
        analysed = analyse(
            newgrid.reshape(field_count, grid_width), own_info[2], own_info[3], own_info[4]
        )
        coeffs = (analysed * (weight * jnp.sqrt(2.0 / own_info[0].astype(jnp.float32)))).astype(
            jnp.bfloat16
        )
        coeffs = coeffs.reshape(1, variables, level_count, 2, orders_total)
        returned = lax.all_to_all(coeffs, "wave", split_axis=4, concat_axis=0, tiled=True)
        spectral_state = jnp.einsum(
            "jvlcs,sjn->vlcsn", returned, masked, preferred_element_type=jnp.float32
        ).astype(jnp.bfloat16)
    return spectral_state


def solution(mesh):
    placed = (
        P(None, "lev", None, "wave", None),
        P("wave", None, None),
        P(),
        P(),
        P("wave"),
        P(None, "lev", None, "wave", None),
        P(None, "lev", None, "wave", None),
        P(None, "lev", None, "wave", None),
    )
    return jax.shard_map(
        per_device,
        mesh=mesh,
        in_specs=placed,
        out_specs=P(None, "lev", None, "wave", None),
        check_vma=False,
    )
```

profile of v0, /device:TPU:0, one launch (start us, length us, event | category | flops | bytes accessed | tf_op | source)
XLA Modules:
  0.0 356.6 jit_solution(9272613454068507887)
XLA Ops:
  2.6 5.7 %fusion.31 = bf16[8,4,1,2,160]{0,1,3,4,2:T(4,128)(2,1)} fusion(bf16[4,2,160,1280]{3,2,1,0:T(8,128)(2,1)S(1)} %bitcast.183, bf16[160,8,1280]{2,1,0:T(8,128)(2,1)} %param.11, pred[160,1280]{1,0:T(8,128)(4,1)S(1)} %iota_compare_fusion), kind=kOutput, calls=%fused_computation.38 | convolution fusion | flops 27863040 | bytes 6778880 | tf_op jit(solution)/shard_map/vlcsn,sjn->jvlcs/dot_general | solution.py:109
  8.3 2.0 copy.155
  10.3 6.4 %all-to-all-start = ((bf16[8,4,1,2,160]{4,1,3,2,0:T(4,128)(2,1)}), bf16[8,4,1,2,160]{4,1,3,2,0:T(4,128)(2,1)S(1)}, u32[]{:S(2)}, u32[]{:S(2)}) async-start(bf16[8,4,1,2,160]{4,1,3,2,0:T(4,128)(2,1)} %copy.155), calls=%async_computation | async-start | bytes 65536 | tf_op jit(solution)/shard_map/all_to_all | solution.py:112
  22.4 36.4 %select_convert_fusion.1 = (bf16[1280,512]{1,0:T(8,128)(2,1)S(1)}, bf16[1280,512]{1,0:T(8,128)(2,1)S(1)}) fusion(f32[]{:T(128)S(6)} %div.18, s32[]{:T(128)S(6)} %select_n.124, s32[1280]{0:T(1024)S(1)} %copy-done.13, pred[1280]{0:T(1024)(128)(4,1)S(1)} %broadcast_compare_fusion, pred[]{:T(512)S(6)} %lt.62), kind=kLoop, calls=%fused_computation.27 | loop fusion | flops 9830400 | bytes 2627849 | tf_op jit(solution)/shard_map/convert.8
  62.5 2.4 collective-permute-start
  66.4 1.7 pad_maximum_fusion
  69.3 4.9 %copy.157 = f32[4,1,3,5632]{0,3,2,1:T(8,128)} copy(f32[4,1,3,5632]{3,0,2,1:T(4,128)S(1)} %maximum_convert_fusion) | data formatting | bytes 540672 | tf_op jit(solution)/shard_map/convert_element_type | solution.py:125
  74.2 78.1 %gather_fusion = f32[22528,4]{1,0:T(8,128)} fusion(f32[4,16896]{0,1:T(8,128)} %bitcast.186, s32[22528]{0:T(1024)S(1)} %fusion.60), kind=kCustom, calls=%fused_computation.clone | custom fusion | bytes 811008 | tf_op jit(solution)/shard_map/jit(_take)/gather | solution.py:131
  152.3 12.9 %broadcast_select_fusion.1 = f32[22528,4]{1,0:T(8,128)S(1)} fusion(f32[22528,4]{1,0:T(8,128)} %gather_fusion, pred[22528]{0:T(1024)(128)(4,1)S(1)} %compare_and_fusion.1), kind=kLoop, calls=%fused_computation.5 | loop fusion | flops 90112 | bytes 743424 | tf_op jit(solution)/shard_map/jit(_take)/select_n | solution.py:131
  165.2 3.9 %multiply_reduce_fusion.1 = f32[4,5632]{0,1:T(8,128)S(1)} fusion(f32[4,1,4,5632]{0,3,2,1:T(8,128)S(1)} %bitcast.185, f32[4,5632]{1,0:T(4,128)S(1)} %copy-done.11), kind=kLoop, calls=%fused_computation.3 | loop fusion | flops 157696 | bytes 540672 | tf_op jit(solution)/shard_map/reduce_sum | solution.py:133
  169.1 2.4 slice_bitcast_fusion.1
  173.1 2.8 copy.159
  177.9 2.1 copy.164
  180.0 2.7 reshape.894
  182.7 12.4 %all_to_all.60 = bf16[8,2,640]{2,1,0:T(2,128)(2,1)} all-to-all(bf16[8,2,640]{2,1,0:T(2,128)(2,1)} %reshape.894), channel_id=1, replica_groups=mesh['wave'=8,'lev'=4] {'wave'}, dimensions={0} | all-to-all | bytes 40960 | tf_op jit(solution)/shard_map/all_to_all | solution.py:145
  195.1 2.9 reshape.895
  198.0 4.0 %copy.166 = bf16[1,4,1,2,8,160]{4,1,3,5,2,0:T(4,128)(2,1)} copy(bf16[1,4,1,2,8,160]{1,3,5,4,2,0:T(2,128)(2,1)} %bitcast.191) | data formatting | bytes 40960 | tf_op jit(solution)/shard_map/all_to_all | solution.py:145
  202.0 6.1 %fusion.36 = bf16[8,4,1,2,160]{0,1,3,4,2:T(4,128)(2,1)} fusion(bf16[160,8,1280]{2,1,0:T(8,128)(2,1)S(1)} %copy-done.8, pred[160,1280]{1,0:T(8,128)(4,1)} %copy-done.9, bf16[1,4,1,2,8,160]{4,1,3,5,2,0:T(4,128)(2,1)} %copy.166), kind=kOutput, calls=%fused_computation.39 | convolution fusion | flops 57354240 | bytes 3522560 | tf_op jit(solution)/shard_map/vlcsn,sjn->jvlcs/dot_general | solution.py:109
  208.1 2.1 copy.167
  210.2 3.5 all-to-all-start.2
  213.8 5.4 %all-to-all-done.2 = bf16[8,4,1,2,160]{4,1,3,2,0:T(4,128)(2,1)S(1)} async-done(((bf16[8,4,1,2,160]{4,1,3,2,0:T(4,128)(2,1)}), bf16[8,4,1,2,160]{4,1,3,2,0:T(4,128)(2,1)S(1)}, u32[]{:S(2)}, u32[]{:S(2)}) %all-to-all-start.2) | async-done | bytes 20512 | tf_op jit(solution)/shard_map/all_to_all | solution.py:112
  224.3 2.3 collective-permute-done.3
  226.7 4.9 %copy.169 = f32[4,1,3,5632]{0,3,2,1:T(8,128)} copy(f32[4,1,3,5632]{3,0,2,1:T(4,128)S(1)} %maximum_convert_fusion.1) | data formatting | bytes 540672 | tf_op jit(solution)/shard_map/convert_element_type | solution.py:125
  231.6 78.1 %gather_fusion.1 = f32[22528,4]{1,0:T(8,128)} fusion(f32[4,16896]{0,1:T(8,128)} %bitcast.187, s32[22528]{0:T(1024)S(1)} %fusion.61), kind=kCustom, calls=%fused_computation.1.clone | custom fusion | bytes 811008 | tf_op jit(solution)/shard_map/jit(_take)/gather | solution.py:131
  309.7 12.9 %broadcast_select_fusion = f32[22528,4]{1,0:T(8,128)S(1)} fusion(f32[22528,4]{1,0:T(8,128)} %gather_fusion.1, pred[22528]{0:T(1024)(128)(4,1)S(1)} %compare_and_fusion), kind=kLoop, calls=%fused_computation.4 | loop fusion | flops 90112 | bytes 743424 | tf_op jit(solution)/shard_map/jit(_take)/select_n | solution.py:131
  322.6 3.9 %multiply_reduce_fusion = f32[4,5632]{0,1:T(8,128)S(1)} fusion(f32[4,1,4,5632]{0,3,2,1:T(8,128)S(1)} %bitcast.184, f32[4,5632]{1,0:T(4,128)S(1)} %copy-done.10), kind=kLoop, calls=%fused_computation.2 | loop fusion | flops 157696 | bytes 540672 | tf_op jit(solution)/shard_map/reduce_sum | solution.py:133
  326.5 2.4 slice_bitcast_fusion
  330.6 2.8 copy.171
  336.3 9.6 %all_to_all.61 = bf16[8,2,640]{2,1,0:T(2,128)(2,1)S(1)} all-to-all(bf16[8,2,640]{2,1,0:T(2,128)(2,1)S(1)} %reshape.896), channel_id=1, replica_groups=mesh['wave'=8,'lev'=4] {'wave'}, dimensions={0} | all-to-all | bytes 40960 | tf_op jit(solution)/shard_map/all_to_all | solution.py:145
  347.2 3.0 copy.179
  350.2 4.0 %fusion.1 = bf16[4,1,2,160,1280]{4,0,2,3,1:T(4,128)(2,1)S(1)} fusion(bf16[160,8,1280]{2,1,0:T(8,128)(2,1)} %param.11, pred[160,1280]{1,0:T(8,128)(4,1)} %copy-done.9, bf16[1,4,1,2,8,160]{4,1,3,5,2,0:T(4,128)(2,1)} %copy.179), kind=kOutput, calls=%fused_computation.10 | convolution fusion | flops 29491200 | bytes 6778880 | tf_op jit(solution)/shard_map/jvlcs,sjn->vlcsn/dot_general | solution.py:146
  354.3 2.3 copy.180
  (97 shorter events, 25.8 us)
Async XLA Ops:
  0.0 1.9 copy-start
  1.9 0.7 copy-start.9
  2.6 14.0 %copy-start.14 = (s32[8]{0:T(128)S(1)}, s32[8]{0:T(128)}, u32[]{:S(2)}) copy-start(s32[8]{0:T(128)} %param.13) | copy-start | bytes 100
  2.6 18.5 %copy-start.13 = (s32[1280]{0:T(1024)S(1)}, s32[1280]{0:T(1024)}, u32[]{:S(2)}) copy-start(s32[1280]{0:T(1024)} %param.12) | copy-start | bytes 15364
  8.3 50.6 %copy-start.12 = (f32[2,1,4,1,5632]{4,3,2,1,0:T(1,128)S(1)}, f32[2,1,4,1,5632]{4,3,2,1,0:T(1,128)}, u32[]{:S(2)}) copy-start(f32[2,1,4,1,5632]{4,3,2,1,0:T(1,128)} %param.17) | copy-start | bytes 540676
  10.3 50.2 %all-to-all-start = ((bf16[8,4,1,2,160]{4,1,3,2,0:T(4,128)(2,1)}), bf16[8,4,1,2,160]{4,1,3,2,0:T(4,128)(2,1)S(1)}, u32[]{:S(2)}, u32[]{:S(2)}) async-start(bf16[8,4,1,2,160]{4,1,3,2,0:T(4,128)(2,1)} %copy.155), calls=%async_computation | async-start | bytes 65536 | tf_op jit(solution)/shard_map/all_to_all | solution.py:112
  58.9 7.5 %copy-start.4 = (bf16[1280,512]{1,0:T(8,128)(2,1)}, bf16[1280,512]{1,0:T(8,128)(2,1)S(1)}, u32[]{:S(2)}) copy-start(bf16[1280,512]{1,0:T(8,128)(2,1)S(1)} %get-tuple-element.26) | copy-start | bytes 3932164
  58.9 7.5 %copy-start.6 = (bf16[1280,512]{1,0:T(8,128)(2,1)}, bf16[1280,512]{1,0:T(8,128)(2,1)S(1)}, u32[]{:S(2)}) copy-start(bf16[1280,512]{1,0:T(8,128)(2,1)S(1)} %get-tuple-element.27) | copy-start | bytes 3932164
  62.5 6.3 %collective-permute-start = (bf16[4,1,1,5632]{3,0,2,1:T(4,128)(2,1)S(1)}, bf16[4,1,1,5632]{3,0,2,1:T(4,128)(2,1)S(1)}, u32[]{:S(2)}, u32[]{:S(2)}) collective-permute-start(bf16[4,1,1,5632]{3,0,2,1:T(4,128)(2,1)S(1)} %select_convert_fusion.3), channel_id=1, source_target_pairs={{0,4},{4,8},{8,12},{12,16},{16,20},{20,24},{24,28},{1,5},{5,9},{9,... | collective-permute-start | bytes 135176 | tf_op jit(solution)/shard_map/ppermute | solution.py:16
  64.9 4.3 %collective-permute-start.1 = (bf16[4,1,1,5632]{3,0,2,1:T(4,128)(2,1)S(1)}, bf16[4,1,1,5632]{3,0,2,1:T(4,128)(2,1)S(1)}, u32[]{:S(2)}, u32[]{:S(2)}) collective-permute-start(bf16[4,1,1,5632]{3,0,2,1:T(4,128)(2,1)S(1)} %select_convert_fusion.3), channel_id=1, source_target_pairs={{4,0},{8,4},{12,8},{16,12},{20,16},{24,20},{28,24},{5,1},{9,5},{13... | collective-permute-start | bytes 135176 | tf_op jit(solution)/shard_map/ppermute | solution.py:19
  152.3 12.9 %copy-start.11 = (f32[4,5632]{1,0:T(4,128)S(1)}, f32[4,5632]{1,0:T(4,128)}, u32[]{:S(2)}) copy-start(f32[4,5632]{1,0:T(4,128)} %get-tuple-element.33) | copy-start | bytes 270340
  173.1 3.1 copy-start.2
  177.1 24.9 %copy-start.8 = (bf16[160,8,1280]{2,1,0:T(8,128)(2,1)S(1)}, bf16[160,8,1280]{2,1,0:T(8,128)(2,1)}, u32[]{:S(2)}) copy-start(bf16[160,8,1280]{2,1,0:T(8,128)(2,1)} %param.11) | copy-start | bytes 9830404
  208.1 12.5 %copy-start.5 = (bf16[1280,512]{1,0:T(8,128)(2,1)S(1)}, bf16[1280,512]{1,0:T(8,128)(2,1)}, u32[]{:S(2)}) copy-start(bf16[1280,512]{1,0:T(8,128)(2,1)} %copy-done.4) | copy-start | bytes 3932164
  208.1 12.5 %copy-start.7 = (bf16[1280,512]{1,0:T(8,128)(2,1)S(1)}, bf16[1280,512]{1,0:T(8,128)(2,1)}, u32[]{:S(2)}) copy-start(bf16[1280,512]{1,0:T(8,128)(2,1)} %copy-done.6) | copy-start | bytes 3932164
  210.2 9.0 %all-to-all-start.2 = ((bf16[8,4,1,2,160]{4,1,3,2,0:T(4,128)(2,1)}), bf16[8,4,1,2,160]{4,1,3,2,0:T(4,128)(2,1)S(1)}, u32[]{:S(2)}, u32[]{:S(2)}) async-start(bf16[8,4,1,2,160]{4,1,3,2,0:T(4,128)(2,1)} %copy.167), calls=%async_computation.2 | async-start | bytes 65536 | tf_op jit(solution)/shard_map/all_to_all | solution.py:112
  221.3 3.0 collective-permute-start.2
  222.9 3.7 %collective-permute-start.3 = (bf16[4,1,1,5632]{3,0,2,1:T(4,128)(2,1)S(1)}, bf16[4,1,1,5632]{3,0,2,1:T(4,128)(2,1)S(1)}, u32[]{:S(2)}, u32[]{:S(2)}) collective-permute-start(bf16[4,1,1,5632]{3,0,2,1:T(4,128)(2,1)S(1)} %select_convert_fusion.2), channel_id=1, source_target_pairs={{4,0},{8,4},{12,8},{16,12},{20,16},{24,20},{28,24},{5,1},{9,5},{13... | collective-permute-start | bytes 135176 | tf_op jit(solution)/shard_map/ppermute | solution.py:19
  309.7 12.9 %copy-start.10 = (f32[4,5632]{1,0:T(4,128)S(1)}, f32[4,5632]{1,0:T(4,128)}, u32[]{:S(2)}) copy-start(f32[4,5632]{1,0:T(4,128)} %get-tuple-element.32) | copy-start | bytes 270340
  330.6 3.1 copy-start.3
  350.2 6.4 %copy-start.1 = (bf16[4,1,2,160,1280]{4,3,2,1,0:T(8,128)(2,1)S(1)}, bf16[4,1,2,160,1280]{4,3,2,1,0:T(8,128)(2,1)}, u32[]{:S(2)}) copy-start(bf16[4,1,2,160,1280]{4,3,2,1,0:T(8,128)(2,1)} %param.10) | copy-start | bytes 9830404
where the time goes:
time: 357 us
  local copies, waits for them, and re-layouts  209 us (59%)
  other arithmetic  78.6 us (22%)
  blocking collectives  22 us (6%)
  matrix products  18.7 us (5%)
  starting transfers between devices  16.7 us (5%)
  waiting for transfers between devices  8.07 us (2%)
  between operations  3.92 us (1%)
    gather x2, local copies, waits for them, and re-layouts, per_device(): values = jnp.take(flat_rows, flat_index, axis=1)  156 us
    another operation x3, other arithmetic  37.4 us
    select_n x2, other arithmetic, per_device(): values = jnp.take(flat_rows, flat_index, axis=1)  25.7 us
    all_to_all x2, blocking collectives, per_device(): lax.all_to_all(coeffs, 'wave', split_axis=4, concat_axis=0, tiled=True)  22 us
    dot_general x2, matrix products, per_device(): jnp.einsum('vlcsn,sjn->jvlcs', spectral_state, masked, preferred_element_...  11.8 us
    unnamed x42, local copies, waits for them, and re-layouts  10.8 us
    concatenate x6, local copies, waits for them, and re-layouts, per_device(): jnp.roll(interp, -1, axis=0)  10.4 us
    all_to_all x2, starting transfers between devices, per_device(): lax.all_to_all(fourier, 'wave', split_axis=0, concat_axis=4, tiled=True)  9.9 us
  transfers between devices with their start and end apart: 6, of which 3 were waited for; matrix products, arithmetic and copies ran while one was open for 12% of the time, Pallas kernels for 0%

commit v1 on v0

--- a/solution.py
+++ b/solution.py
@@ -6,6 +6,12 @@
 
 BLOCK = 512
 full_turn = 2.0 * math.pi
+
+
+def exchange_blocks(value, name, split, join):
+    pieces = jnp.split(value, lax.axis_size(name), axis=split)
+    received = lax.all_to_all(jnp.stack(pieces), name, 0, 0)
+    return jnp.concatenate(received, axis=join)
 
 
 def extended_2(block, sides, width):
@@ -142,7 +148,7 @@
             jnp.bfloat16
         )
         coeffs = coeffs.reshape(1, variables, level_count, 2, orders_total)
-        returned = lax.all_to_all(coeffs, "wave", split_axis=4, concat_axis=0, tiled=True)
+        returned = exchange_blocks(coeffs, "wave", 4, 0)
         spectral_state = jnp.einsum(
             "jvlcs,sjn->vlcsn", returned, masked, preferred_element_type=jnp.float32
         ).astype(jnp.bfloat16)

time: 357 us -> 344 us (0.964)
  local copies, waits for them, and re-layouts: 209 us -> 194 us
    unnamed x42 -> x54, local copies, waits for them, and re-layouts: 10.8 us -> 3.74 us
    all_to_all x2, local copies, waits for them, and re-layouts: 6.97 us -> 1.2 us  [exchange_blocks(): received = lax.all_to_all(jnp.stack(pieces), name, 0, 0)]
where the time goes in v1:
time: 344 us; the launch traced here: 343 us
  local copies, waits for them, and re-layouts  194 us (56%)
  other arithmetic  77.9 us (23%)
  blocking collectives  21.8 us (6%)
  matrix products  20.5 us (6%)
  starting transfers between devices  16.7 us (5%)
  waiting for transfers between devices  8.07 us (2%)
  between operations  4.06 us (1%)
    gather x2, local copies, waits for them, and re-layouts, per_device(): values = jnp.take(flat_rows, flat_index, axis=1)  157 us
    another operation x3, other arithmetic  37.4 us
    select_n x2, other arithmetic, per_device(): values = jnp.take(flat_rows, flat_index, axis=1)  25.7 us
    all_to_all x2, blocking collectives, exchange_blocks(): received = lax.all_to_all(jnp.stack(pieces), name, 0, 0)  21.8 us
    dot_general x2, matrix products, per_device(): jnp.einsum('vlcsn,sjn->jvlcs', spectral_state, masked, preferred_element_...  13.5 us
    concatenate x6, local copies, waits for them, and re-layouts, per_device(): jnp.roll(interp, -1, axis=0)  10.4 us
    convert_element_type x2, local copies, waits for them, and re-layouts, per_device(): extended = extended_2(own_grid.reshape(variables, level_count, 1, grid_wi...  9.9 us
    all_to_all x2, starting transfers between devices, per_device(): lax.all_to_all(fourier, 'wave', split_axis=0, concat_axis=4, tiled=True)  9.69 us
  transfers between devices with their start and end apart: 6, of which 3 were waited for; matrix products, arithmetic and copies ran while one was open for 12% of the time, Pallas kernels for 0%

profile of v1, /device:TPU:0, one launch (start us, length us, event | category | flops | bytes accessed | tf_op | source)
XLA Modules:
  0.0 343.3 jit_solution(4692406887781137849)
XLA Ops:
  2.7 5.7 %fusion.31 = bf16[8,4,1,2,160]{0,1,3,4,2:T(4,128)(2,1)} fusion(bf16[4,2,160,1280]{3,2,1,0:T(8,128)(2,1)S(1)} %bitcast.233, bf16[160,8,1280]{2,1,0:T(8,128)(2,1)} %param.11, pred[160,1280]{1,0:T(8,128)(4,1)S(1)} %iota_compare_fusion), kind=kOutput, calls=%fused_computation.38 | convolution fusion | flops 27863040 | bytes 6778880 | tf_op jit(solution)/shard_map/vlcsn,sjn->jvlcs/dot_general | solution.py:115
  8.3 2.0 copy.631
  10.3 6.4 %all-to-all-start = ((bf16[8,4,1,2,160]{4,1,3,2,0:T(4,128)(2,1)}), bf16[8,4,1,2,160]{4,1,3,2,0:T(4,128)(2,1)S(1)}, u32[]{:S(2)}, u32[]{:S(2)}) async-start(bf16[8,4,1,2,160]{4,1,3,2,0:T(4,128)(2,1)} %copy.631), calls=%async_computation | async-start | bytes 65536 | tf_op jit(solution)/shard_map/all_to_all | solution.py:118
  19.2 1.2 slice_add_fusion
  21.2 1.2 fusion.57
  22.4 36.4 %select_convert_fusion.1 = (bf16[1280,512]{1,0:T(8,128)(2,1)S(1)}, bf16[1280,512]{1,0:T(8,128)(2,1)S(1)}) fusion(f32[]{:T(128)S(6)} %div.18, s32[]{:T(128)S(6)} %select_n.124, s32[1280]{0:T(1024)S(1)} %copy-done.14, pred[1280]{0:T(1024)(128)(4,1)S(1)} %broadcast_compare_fusion, pred[]{:T(512)S(6)} %lt.62), kind=kLoop, calls=%fused_computation.27 | loop fusion | flops 9830400 | bytes 2627849 | tf_op jit(solution)/shard_map/convert.8
  62.5 2.4 collective-permute-start
  64.9 1.5 collective-permute-start.1
  66.4 1.7 pad_maximum_fusion
  69.3 4.9 %copy.633 = f32[4,1,3,5632]{0,3,2,1:T(8,128)} copy(f32[4,1,3,5632]{3,0,2,1:T(4,128)S(1)} %maximum_convert_fusion) | data formatting | bytes 540672 | tf_op jit(solution)/shard_map/convert_element_type | solution.py:131
  74.2 78.5 %gather_fusion = f32[22528,4]{1,0:T(8,128)} fusion(f32[4,16896]{0,1:T(8,128)} %bitcast.236, s32[22528]{0:T(1024)S(1)} %fusion.60), kind=kCustom, calls=%fused_computation.clone | custom fusion | bytes 811008 | tf_op jit(solution)/shard_map/jit(_take)/gather | solution.py:137
  152.7 12.9 %broadcast_select_fusion.1 = f32[22528,4]{1,0:T(8,128)S(1)} fusion(f32[22528,4]{1,0:T(8,128)} %gather_fusion, pred[22528]{0:T(1024)(128)(4,1)S(1)} %compare_and_fusion.1), kind=kLoop, calls=%fused_computation.5 | loop fusion | flops 90112 | bytes 743424 | tf_op jit(solution)/shard_map/jit(_take)/select_n | solution.py:137
  165.6 3.9 %multiply_reduce_fusion.1 = f32[4,5632]{0,1:T(8,128)S(1)} fusion(f32[4,1,4,5632]{0,3,2,1:T(8,128)S(1)} %bitcast.235, f32[4,5632]{1,0:T(4,128)S(1)} %copy-done.11), kind=kLoop, calls=%fused_computation.3 | loop fusion | flops 157696 | bytes 540672 | tf_op jit(solution)/shard_map/reduce_sum | solution.py:139
  169.5 2.4 slice_bitcast_fusion.1
  173.6 2.8 copy.635
  178.4 12.2 %all_to_all.40 = bf16[8,1,4,1,2,160]{5,2,4,3,1,0:T(4,128)(2,1)S(1)} all-to-all(bf16[8,1,4,1,2,160]{5,2,4,3,1,0:T(4,128)(2,1)S(1)} %copy.640), channel_id=1, replica_groups=mesh['wave'=8,'lev'=4] {'wave'}, dimensions={0} | all-to-all | bytes 40960 | tf_op jit(solution)/shard_map/all_to_all | solution.py:13
  190.8 7.9 %fusion.36 = bf16[8,4,1,2,160]{0,1,3,4,2:T(4,128)(2,1)} fusion(bf16[160,8,1280]{2,1,0:T(8,128)(2,1)} %param.11, pred[160,1280]{1,0:T(8,128)(4,1)S(1)} %copy-done.9, bf16[8,1,4,1,2,160]{0,2,4,5,3,1:T(4,128)(2,1)S(1)} %copy.641), kind=kOutput, calls=%fused_computation.39 | convolution fusion | flops 57354240 | bytes 3522560 | tf_op jit(solution)/shard_map/vlcsn,sjn->jvlcs/dot_general | solution.py:115
  198.7 2.1 copy.642
  200.7 3.3 all-to-all-start.2
  204.1 5.6 %all-to-all-done.2 = bf16[8,4,1,2,160]{4,1,3,2,0:T(4,128)(2,1)S(1)} async-done(((bf16[8,4,1,2,160]{4,1,3,2,0:T(4,128)(2,1)}), bf16[8,4,1,2,160]{4,1,3,2,0:T(4,128)(2,1)S(1)}, u32[]{:S(2)}, u32[]{:S(2)}) %all-to-all-start.2) | async-done | bytes 20512 | tf_op jit(solution)/shard_map/all_to_all | solution.py:118
  211.8 1.6 collective-permute-start.2
  213.5 1.5 collective-permute-start.3
  215.1 2.1 collective-permute-done.3
  217.3 4.9 %copy.644 = f32[4,1,3,5632]{0,3,2,1:T(8,128)} copy(f32[4,1,3,5632]{3,0,2,1:T(4,128)S(1)} %maximum_convert_fusion.1) | data formatting | bytes 540672 | tf_op jit(solution)/shard_map/convert_element_type | solution.py:131
  222.2 78.5 %gather_fusion.1 = f32[22528,4]{1,0:T(8,128)} fusion(f32[4,16896]{0,1:T(8,128)} %bitcast.237, s32[22528]{0:T(1024)S(1)} %fusion.61), kind=kCustom, calls=%fused_computation.1.clone | custom fusion | bytes 811008 | tf_op jit(solution)/shard_map/jit(_take)/gather | solution.py:137
  300.7 12.9 %broadcast_select_fusion = f32[22528,4]{1,0:T(8,128)S(1)} fusion(f32[22528,4]{1,0:T(8,128)} %gather_fusion.1, pred[22528]{0:T(1024)(128)(4,1)S(1)} %compare_and_fusion), kind=kLoop, calls=%fused_computation.4 | loop fusion | flops 90112 | bytes 743424 | tf_op jit(solution)/shard_map/jit(_take)/select_n | solution.py:137
  313.6 3.9 %multiply_reduce_fusion = f32[4,5632]{0,1:T(8,128)S(1)} fusion(f32[4,1,4,5632]{0,3,2,1:T(8,128)S(1)} %bitcast.234, f32[4,5632]{1,0:T(4,128)S(1)} %copy-done.10), kind=kLoop, calls=%fused_computation.2 | loop fusion | flops 157696 | bytes 540672 | tf_op jit(solution)/shard_map/reduce_sum | solution.py:139
  317.5 2.4 slice_bitcast_fusion
  321.5 2.8 copy.646
  326.3 9.6 %all_to_all.41 = bf16[8,1,4,1,2,160]{5,2,4,3,1,0:T(4,128)(2,1)S(1)} all-to-all(bf16[8,1,4,1,2,160]{5,2,4,3,1,0:T(4,128)(2,1)S(1)} %copy.652), channel_id=1, replica_groups=mesh['wave'=8,'lev'=4] {'wave'}, dimensions={0} | all-to-all | bytes 40960 | tf_op jit(solution)/shard_map/all_to_all | solution.py:13
  336.9 4.0 %fusion.1 = bf16[4,1,2,160,1280]{4,0,2,3,1:T(4,128)(2,1)S(1)} fusion(bf16[160,8,1280]{2,1,0:T(8,128)(2,1)} %param.11, pred[160,1280]{1,0:T(8,128)(4,1)} %copy-done.8, bf16[8,1,4,1,2,160]{0,2,4,5,3,1:T(4,128)(2,1)} %copy.653), kind=kOutput, calls=%fused_computation.10 | convolution fusion | flops 29491200 | bytes 6778880 | tf_op jit(solution)/shard_map/jvlcs,sjn->vlcsn/dot_general | solution.py:152
  341.0 2.3 copy.654
  (115 shorter events, 17.8 us)
Async XLA Ops:
  0.0 1.9 copy-start
  1.9 0.7 copy-start.8
  2.6 14.0 %copy-start.15 = (s32[8]{0:T(128)S(1)}, s32[8]{0:T(128)}, u32[]{:S(2)}) copy-start(s32[8]{0:T(128)} %param.13) | copy-start | bytes 100
  2.6 16.6 %copy-start.12 = (s32[2,1,4,1,5632]{4,3,2,1,0:T(1,128)S(1)}, s32[2,1,4,1,5632]{4,3,2,1,0:T(1,128)}, u32[]{:S(2)}) copy-start(s32[2,1,4,1,5632]{4,3,2,1,0:T(1,128)} %param.16) | copy-start | bytes 540676
  2.7 18.5 %copy-start.14 = (s32[1280]{0:T(1024)S(1)}, s32[1280]{0:T(1024)}, u32[]{:S(2)}) copy-start(s32[1280]{0:T(1024)} %param.12) | copy-start | bytes 15364
  8.3 50.5 %copy-start.13 = (f32[2,1,4,1,5632]{4,3,2,1,0:T(1,128)S(1)}, f32[2,1,4,1,5632]{4,3,2,1,0:T(1,128)}, u32[]{:S(2)}) copy-start(f32[2,1,4,1,5632]{4,3,2,1,0:T(1,128)} %param.17) | copy-start | bytes 540676
  10.3 50.1 %all-to-all-start = ((bf16[8,4,1,2,160]{4,1,3,2,0:T(4,128)(2,1)}), bf16[8,4,1,2,160]{4,1,3,2,0:T(4,128)(2,1)S(1)}, u32[]{:S(2)}, u32[]{:S(2)}) async-start(bf16[8,4,1,2,160]{4,1,3,2,0:T(4,128)(2,1)} %copy.631), calls=%async_computation | async-start | bytes 65536 | tf_op jit(solution)/shard_map/all_to_all | solution.py:118
  58.9 7.5 %copy-start.4 = (bf16[1280,512]{1,0:T(8,128)(2,1)}, bf16[1280,512]{1,0:T(8,128)(2,1)S(1)}, u32[]{:S(2)}) copy-start(bf16[1280,512]{1,0:T(8,128)(2,1)S(1)} %get-tuple-element.26) | copy-start | bytes 3932164
  58.9 7.5 %copy-start.6 = (bf16[1280,512]{1,0:T(8,128)(2,1)}, bf16[1280,512]{1,0:T(8,128)(2,1)S(1)}, u32[]{:S(2)}) copy-start(bf16[1280,512]{1,0:T(8,128)(2,1)S(1)} %get-tuple-element.27) | copy-start | bytes 3932164
  62.5 6.3 %collective-permute-start = (bf16[4,1,1,5632]{3,0,2,1:T(4,128)(2,1)S(1)}, bf16[4,1,1,5632]{3,0,2,1:T(4,128)(2,1)S(1)}, u32[]{:S(2)}, u32[]{:S(2)}) collective-permute-start(bf16[4,1,1,5632]{3,0,2,1:T(4,128)(2,1)S(1)} %select_convert_fusion.3), channel_id=1, source_target_pairs={{0,4},{4,8},{8,12},{12,16},{16,20},{20,24},{24,28},{1,5},{5,9},{9,... | collective-permute-start | bytes 135176 | tf_op jit(solution)/shard_map/ppermute | solution.py:22
  64.9 4.3 %collective-permute-start.1 = (bf16[4,1,1,5632]{3,0,2,1:T(4,128)(2,1)S(1)}, bf16[4,1,1,5632]{3,0,2,1:T(4,128)(2,1)S(1)}, u32[]{:S(2)}, u32[]{:S(2)}) collective-permute-start(bf16[4,1,1,5632]{3,0,2,1:T(4,128)(2,1)S(1)} %select_convert_fusion.3), channel_id=1, source_target_pairs={{4,0},{8,4},{12,8},{16,12},{20,16},{24,20},{28,24},{5,1},{9,5},{13... | collective-permute-start | bytes 135176 | tf_op jit(solution)/shard_map/ppermute | solution.py:25
  152.7 12.9 %copy-start.11 = (f32[4,5632]{1,0:T(4,128)S(1)}, f32[4,5632]{1,0:T(4,128)}, u32[]{:S(2)}) copy-start(f32[4,5632]{1,0:T(4,128)} %get-tuple-element.33) | copy-start | bytes 270340
  173.6 3.1 copy-start.2
  176.6 14.2 %copy-start.9 = (pred[160,1280]{1,0:T(8,128)(4,1)S(1)}, pred[160,1280]{1,0:T(8,128)(4,1)}, u32[]{:S(2)}) copy-start(pred[160,1280]{1,0:T(8,128)(4,1)} %copy-done.8) | copy-start | bytes 614404
  198.7 12.5 %copy-start.5 = (bf16[1280,512]{1,0:T(8,128)(2,1)S(1)}, bf16[1280,512]{1,0:T(8,128)(2,1)}, u32[]{:S(2)}) copy-start(bf16[1280,512]{1,0:T(8,128)(2,1)} %copy-done.4) | copy-start | bytes 3932164
  198.7 12.5 %copy-start.7 = (bf16[1280,512]{1,0:T(8,128)(2,1)S(1)}, bf16[1280,512]{1,0:T(8,128)(2,1)}, u32[]{:S(2)}) copy-start(bf16[1280,512]{1,0:T(8,128)(2,1)} %copy-done.6) | copy-start | bytes 3932164
  200.7 9.0 %all-to-all-start.2 = ((bf16[8,4,1,2,160]{4,1,3,2,0:T(4,128)(2,1)}), bf16[8,4,1,2,160]{4,1,3,2,0:T(4,128)(2,1)S(1)}, u32[]{:S(2)}, u32[]{:S(2)}) async-start(bf16[8,4,1,2,160]{4,1,3,2,0:T(4,128)(2,1)} %copy.642), calls=%async_computation.2 | async-start | bytes 65536 | tf_op jit(solution)/shard_map/all_to_all | solution.py:118
  211.8 3.2 collective-permute-start.2
  213.5 3.7 %collective-permute-start.3 = (bf16[4,1,1,5632]{3,0,2,1:T(4,128)(2,1)S(1)}, bf16[4,1,1,5632]{3,0,2,1:T(4,128)(2,1)S(1)}, u32[]{:S(2)}, u32[]{:S(2)}) collective-permute-start(bf16[4,1,1,5632]{3,0,2,1:T(4,128)(2,1)S(1)} %select_convert_fusion.2), channel_id=1, source_target_pairs={{4,0},{8,4},{12,8},{16,12},{20,16},{24,20},{28,24},{5,1},{9,5},{13... | collective-permute-start | bytes 135176 | tf_op jit(solution)/shard_map/ppermute | solution.py:25
  300.7 12.9 %copy-start.10 = (f32[4,5632]{1,0:T(4,128)S(1)}, f32[4,5632]{1,0:T(4,128)}, u32[]{:S(2)}) copy-start(f32[4,5632]{1,0:T(4,128)} %get-tuple-element.32) | copy-start | bytes 270340
  321.5 3.1 copy-start.3
  336.9 6.4 %copy-start.1 = (bf16[4,1,2,160,1280]{4,3,2,1,0:T(8,128)(2,1)S(1)}, bf16[4,1,2,160,1280]{4,3,2,1,0:T(8,128)(2,1)}, u32[]{:S(2)}) copy-start(bf16[4,1,2,160,1280]{4,3,2,1,0:T(8,128)(2,1)} %param.10) | copy-start | bytes 9830404
